TPU v7x, 32 devices: a whole 2x2x4 slice. The times are simulated.
32 devices in a mesh: wide: 8 (over z, x), narrow: 4 (over y, core).
Axes of the slice: x: 2, y: 2, z: 4, core: 2. Of those that a mesh axis runs over, the one named last changes fastest.
Arguments:
- embeddings: bfloat16 [8192, 512], P(('wide', 'narrow')), may hold values from -26 to 26
- partners: int32 [32, 7], P(('wide', 'narrow')), may hold values from -1 to 7, as said below
- pair_kind: int32 [32, 7], P(('wide', 'narrow')), may hold values from 0 to 1, as said below
- neighbors: int32 [7, 15, 8192], P(None, None, ('wide', 'narrow')), may hold values from 0 to 255
Outputs:
- gradient: float32 [8192, 512], P(('wide', 'narrow'))
- mean_loss: float32 [], replicated
Inputs may be any that keep to these rules, and one draw needn't show every extreme that they name: Row w * 4 + n lists the wide indices of that block's partners in ascending order, then -1 in the remaining slots; a partner has the same narrow index n, is never the block itself, appears once, and the pairing is mutual. In every narrow index one block is paired with all 7 others. `pair_kind`: 1 marks a graph pair, 0 a sampled negative or an empty slot; both directions of a pair carry the same mark, and every block has at least one graph pair.
All inputs are finite; a program needn't handle non-finite values.
Results may differ from a plain program's by a relative error of at most 0.0004.
Values may be sent and summed in bfloat16 or wider, within the bound.
No kernel may reach another device: no remote copies, remote signals or barrier semaphores. Data moves between devices by JAX's collectives and lax.ppermute only.
A program may use at most 64 MiB of HBM per device.

v0:
```python
import jax
import jax.numpy as jnp
from jax import lax
from jax.sharding import PartitionSpec as P


def tile_kernel(local_rows, remote_rows, local_norms, features):
    remote_norms = jnp.sum(jnp.square(remote_rows.astype(jnp.float32)), axis=1)
    inner = jnp.einsum("id,jd->ij", local_rows, remote_rows, preferred_element_type=jnp.float32)
    distance = local_norms[:, None] + remote_norms[None, :] - 2.0 * inner
    return 1.0 / (1.0 + distance / features)


def edge_counts(targets, block_rows):
    columns = lax.broadcasted_iota(jnp.int32, (1, 1, block_rows), 2)
    return jnp.sum((targets[:, :, None] == columns).astype(jnp.float32), axis=0)


def mirrored_counts(sources, block_rows):
    rows_index = lax.broadcasted_iota(jnp.int32, (1, block_rows, 1), 1)
    return jnp.sum((sources[:, None, :] == rows_index).astype(jnp.float32), axis=0)


def per_device(embeddings, partners, pair_kind, neighbors):
    block_rows, features = embeddings.shape
    slot_count = partners.shape[1]
    groups = lax.axis_size("wide")
    column = lax.all_gather(embeddings, "wide", axis=0, tiled=True).reshape(
        groups, block_rows, features
    )
    local_float = embeddings.astype(jnp.float32)
    local_norms = jnp.sum(jnp.square(local_float), axis=1)
    partner_row = partners[0]
    mark_row = pair_kind[0].astype(jnp.float32)

    def remote_of(slot):
        partner = partner_row[slot]
        return (
            partner,
            lax.dynamic_index_in_dim(column, jnp.maximum(partner, 0), 0, keepdims=False),
        )

    def first(slot, carry):

        def first_active(carry):
            sums, kernels, counts_store = carry
            partner, remote_rows = remote_of(slot)
            kernel = tile_kernel(embeddings, remote_rows, local_norms, features)
            targets = lax.dynamic_index_in_dim(neighbors, slot, 0, keepdims=False)
            counts = edge_counts(targets, block_rows) * mark_row[slot]
            sums = (
                sums[0] + jnp.sum(kernel),
                sums[1] + jnp.sum(counts * jnp.log(kernel)),
                sums[2] + jnp.sum(counts),
                sums[3] + float(block_rows * block_rows),
            )
            kernels = lax.dynamic_update_index_in_dim(kernels, kernel, slot, 0)
            counts_store = lax.dynamic_update_index_in_dim(counts_store, counts, slot, 0)
            return (sums, kernels, counts_store)

        return lax.cond(partner_row[slot] >= 0, first_active, lambda carry: carry, carry)

    nothing = jnp.zeros((), jnp.float32)
    empty_tiles = jnp.zeros((slot_count, block_rows, block_rows), jnp.float32)
    sums, kernels, counts_store = lax.fori_loop(
        0, slot_count, first, ((nothing, nothing, nothing, nothing), empty_tiles, empty_tiles)
    )
    kernel_sum, attract_sum, edge_sum, entry_sum = sums
    total, attract, edges_total, entries = lax.psum(
        (kernel_sum, attract_sum, edge_sum, entry_sum), ("wide", "narrow")
    )
    mean_loss = -attract / edges_total + jnp.log(total / entries)
    repulsion = edges_total / total
    start_gradient = jnp.zeros((block_rows, features), jnp.float32)
    selector = (partner_row[None, :] == lax.broadcasted_iota(jnp.int32, (groups, 1), 0)).astype(
        jnp.int32
    )
    outgoing = jnp.tensordot(selector, neighbors, axes=1)
    incoming = lax.all_to_all(outgoing, "wide", split_axis=0, concat_axis=0, tiled=True)

    def second(slot, gradient):

        def second_active(gradient):
            partner, remote_rows = remote_of(slot)
            kernel = lax.dynamic_index_in_dim(kernels, slot, 0, keepdims=False)
            counts = lax.dynamic_index_in_dim(counts_store, slot, 0, keepdims=False)
            sources = lax.dynamic_index_in_dim(incoming, jnp.maximum(partner, 0), 0, keepdims=False)
            back_counts = mirrored_counts(sources, block_rows) * mark_row[slot]
            weight = (counts * kernel - repulsion * kernel * kernel) / features
            mirror = (back_counts * kernel - repulsion * kernel * kernel) / features
            row_total = jnp.sum(weight, axis=1) + jnp.sum(mirror, axis=1)
            product = jnp.dot(
                weight.astype(jnp.bfloat16), remote_rows, preferred_element_type=jnp.float32
            ) + jnp.dot(
                mirror.astype(jnp.bfloat16), remote_rows, preferred_element_type=jnp.float32
            )
            return gradient + 2.0 * (row_total[:, None] * local_float - product)

        return lax.cond(partner_row[slot] >= 0, second_active, lambda gradient: gradient, gradient)

    gradient = lax.fori_loop(0, slot_count, second, start_gradient)
    return (gradient, mean_loss)


def solution(mesh):
    in_specs = (
        P(("wide", "narrow"), None),
        P(("wide", "narrow"), None),
        P(("wide", "narrow"), None),
        P(None, None, ("wide", "narrow")),
    )
    out_specs = (P(("wide", "narrow"), None), P())
    return jax.shard_map(
        per_device, mesh=mesh, in_specs=in_specs, out_specs=out_specs, check_vma=False
    )
```

profile of v0, /device:TPU:0, one launch (start us, length us, event | category | flops | bytes accessed | tf_op | source)
XLA Modules:
  0.0 261.6 jit_solution(13438871651944459247)
XLA Ops:
  7.9 1.2 fusion.38
  9.8 7.3 %all-to-all-start = ((s32[8,15,256]{2,1,0:T(8,128)}), s32[8,15,256]{2,1,0:T(8,128)S(1)}, u32[]{:S(2)}, u32[]{:S(2)}) async-start(s32[8,15,256]{2,1,0:T(8,128)} %copy.16), calls=%async_computation | async-start | bytes 262144 | tf_op jit(solution)/shard_map/all_to_all | solution.py:79
  18.2 43.7 %all-gather.2.cloned.1.call-done = bf16[2048,512]{1,0:T(8,128)(2,1)} async-done(((bf16[256,512]{1,0:T(8,128)(2,1)}), bf16[2048,512]{1,0:T(8,128)(2,1)}) %all-gather.2.cloned.1.call-update) | async-done | bytes 2097168 | tf_op jit(solution)/shard_map/all_gather | solution.py:28
  62.1 1.4 broadcast_in_dim.17.clone
  63.5 80.1 %while.39 = (s32[]{:T(128)}, f32[]{:T(128)}, f32[]{:T(128)}, f32[]{:T(128)}, f32[]{:T(128)}, /*index=5*/f32[7,256,256]{1,2,0:T(8,128)S(1)}, f32[7,256,256]{1,2,0...) while((s32[]{:T(128)}, f32[]{:T(128)}, f32[]{:T(128)}, ...), condition=%wide.region_9.10_spmd, body=%wide.region_1.9_spmd.sunk | while | flops 71171840 | bytes 3196933 | solution.py:65
  64.8 10.2 %conditional.4 = ((f32[]{:T(128)}, f32[]{:T(128)}, f32[]{:T(128)}, f32[]{:T(128)}, f32[7,256,256]{1,2,0:T(8,128)S(1)}, /*index=5*/f32[7,256,256]{1,2,0:T(8,128)})) conditional(s32[]{:T(128)} %bitcast.84, (f32[]{:T(128)}, f32[]{:T(128)}, f32[]{:T(128)}, f32[]{:T(128)}, f32[7,256,256]{1,2,0:T(8,128)S(1)}, ...), branch_computations={%region_2.0_spmd, %region_3.8_spmd} | conditional | flops 71171840 | bytes 3196614 | solution.py:61
  65.9 1.1 multiply_reduce_fusion
  69.3 2.6 multiply_reduce_fusion.2
  71.8 1.4 bitcast_dynamic-update-slice_fusion
  76.2 10.2 %conditional.4 = ((f32[]{:T(128)}, f32[]{:T(128)}, f32[]{:T(128)}, f32[]{:T(128)}, f32[7,256,256]{1,2,0:T(8,128)S(1)}, /*index=5*/f32[7,256,256]{1,2,0:T(8,128)})) conditional(s32[]{:T(128)} %bitcast.84, (f32[]{:T(128)}, f32[]{:T(128)}, f32[]{:T(128)}, f32[]{:T(128)}, f32[7,256,256]{1,2,0:T(8,128)S(1)}, ...), branch_computations={%region_2.0_spmd, %region_3.8_spmd} | conditional | flops 71171840 | bytes 3196614 | solution.py:61
  77.4 1.1 multiply_reduce_fusion
  80.7 2.5 multiply_reduce_fusion.2
  83.3 1.3 bitcast_dynamic-update-slice_fusion
  87.6 10.2 %conditional.4 = ((f32[]{:T(128)}, f32[]{:T(128)}, f32[]{:T(128)}, f32[]{:T(128)}, f32[7,256,256]{1,2,0:T(8,128)S(1)}, /*index=5*/f32[7,256,256]{1,2,0:T(8,128)})) conditional(s32[]{:T(128)} %bitcast.84, (f32[]{:T(128)}, f32[]{:T(128)}, f32[]{:T(128)}, f32[]{:T(128)}, f32[7,256,256]{1,2,0:T(8,128)S(1)}, ...), branch_computations={%region_2.0_spmd, %region_3.8_spmd} | conditional | flops 71171840 | bytes 3196614 | solution.py:61
  88.8 1.1 multiply_reduce_fusion
  92.1 2.5 multiply_reduce_fusion.2
  94.7 1.4 bitcast_dynamic-update-slice_fusion
  99.1 10.2 %conditional.4 = ((f32[]{:T(128)}, f32[]{:T(128)}, f32[]{:T(128)}, f32[]{:T(128)}, f32[7,256,256]{1,2,0:T(8,128)S(1)}, /*index=5*/f32[7,256,256]{1,2,0:T(8,128)})) conditional(s32[]{:T(128)} %bitcast.84, (f32[]{:T(128)}, f32[]{:T(128)}, f32[]{:T(128)}, f32[]{:T(128)}, f32[7,256,256]{1,2,0:T(8,128)S(1)}, ...), branch_computations={%region_2.0_spmd, %region_3.8_spmd} | conditional | flops 71171840 | bytes 3196614 | solution.py:61
  100.2 1.1 multiply_reduce_fusion
  103.6 2.5 multiply_reduce_fusion.2
  106.1 1.4 bitcast_dynamic-update-slice_fusion
  110.5 10.2 %conditional.4 = ((f32[]{:T(128)}, f32[]{:T(128)}, f32[]{:T(128)}, f32[]{:T(128)}, f32[7,256,256]{1,2,0:T(8,128)S(1)}, /*index=5*/f32[7,256,256]{1,2,0:T(8,128)})) conditional(s32[]{:T(128)} %bitcast.84, (f32[]{:T(128)}, f32[]{:T(128)}, f32[]{:T(128)}, f32[]{:T(128)}, f32[7,256,256]{1,2,0:T(8,128)S(1)}, ...), branch_computations={%region_2.0_spmd, %region_3.8_spmd} | conditional | flops 71171840 | bytes 3196614 | solution.py:61
  111.7 1.1 multiply_reduce_fusion
  115.0 2.5 multiply_reduce_fusion.2
  117.6 1.4 bitcast_dynamic-update-slice_fusion
  122.0 10.2 %conditional.4 = ((f32[]{:T(128)}, f32[]{:T(128)}, f32[]{:T(128)}, f32[]{:T(128)}, f32[7,256,256]{1,2,0:T(8,128)S(1)}, /*index=5*/f32[7,256,256]{1,2,0:T(8,128)})) conditional(s32[]{:T(128)} %bitcast.84, (f32[]{:T(128)}, f32[]{:T(128)}, f32[]{:T(128)}, f32[]{:T(128)}, f32[7,256,256]{1,2,0:T(8,128)S(1)}, ...), branch_computations={%region_2.0_spmd, %region_3.8_spmd} | conditional | flops 71171840 | bytes 3196614 | solution.py:61
  126.5 2.6 multiply_reduce_fusion.2
  129.0 1.4 bitcast_dynamic-update-slice_fusion
  133.4 10.2 %conditional.4 = ((f32[]{:T(128)}, f32[]{:T(128)}, f32[]{:T(128)}, f32[]{:T(128)}, f32[7,256,256]{1,2,0:T(8,128)S(1)}, /*index=5*/f32[7,256,256]{1,2,0:T(8,128)})) conditional(s32[]{:T(128)} %bitcast.84, (f32[]{:T(128)}, f32[]{:T(128)}, f32[]{:T(128)}, f32[]{:T(128)}, f32[7,256,256]{1,2,0:T(8,128)S(1)}, ...), branch_computations={%region_2.0_spmd, %region_3.8_spmd} | conditional | flops 71171840 | bytes 3196614 | solution.py:61
  134.6 1.1 multiply_reduce_fusion
  137.9 2.5 multiply_reduce_fusion.2
  140.5 1.4 bitcast_dynamic-update-slice_fusion
  143.6 41.4 %all-reduce = (f32[]{:T(128)}, f32[]{:T(128)}, f32[]{:T(128)}, f32[]{:T(128)}) all-reduce(f32[]{:T(128)} %get-tuple-element.499, f32[]{:T(128)} %get-tuple-element.500, f32[]{:T(128)} %get-tuple-element.502, f32[]{:T(128)} %get-tuple-element.503), channel_id=1, replica_groups=mesh['wide'=8,'narrow'=4] {'wide','narrow'}, use_global_device_ids=true, to_apply=%region_10.11 | all-reduce | flops 4 | bytes 32 | tf_op jit(solution)/shard_map/psum | solution.py:69
  189.0 2.7 %copy.17 = f32[7,256,256]{2,1,0:T(8,128)} copy(f32[7,256,256]{1,2,0:T(8,128)} %get-tuple-element.527) | data formatting | bytes 3670016 | tf_op jit(solution)/shard_map/while | solution.py:101
  191.7 1.8 copy.18
  193.6 59.2 %while.40 = (s32[]{:T(128)}, f32[256,512]{1,0:T(8,128)S(1)}, s32[7]{0:T(128)S(1)}, f32[7,256,256]{2,1,0:T(8,128)}, f32[7,256,256]{2,1,0:T(8,128)S(1)}, /*index=5...) while((s32[]{:T(128)}, f32[256,512]{1,0:T(8,128)S(1)}, ...), condition=%wide.region_18.19_spmd, body=%wide.region_12.18_spmd.sunk | while | flops 139329280 | bytes 5297989 | solution.py:101
  194.9 7.2 %conditional.5 = (f32[256,512]{1,0:T(8,128)S(1)}) conditional(s32[]{:T(128)} %bitcast.85, f32[256,512]{1,0:T(8,128)S(1)} %get-tuple-element.814, (s32[]{:T(128)}, f32[7,256,256]{2,1,0:T(8,128)}, f32[7,256,256]{2,1,0:T(8,128)S(1)}, f32[]{:T(128)}, s32[7]{0:T(128)S(1)}, /*index=5*/s32[8,15,256]{2,1,0:T(8,128)S(1)}, f32[7]{0:T(128)S(1)}, ...), branch_computations={%region_13.13_spmd, %region_14.17_spmd} | conditional | flops 139329280 | bytes 5297766 | solution.py:99
  197.2 1.7 fusion.22
  199.0 1.3 fusion.15
  200.3 1.8 fusion.10
  203.3 7.2 %conditional.5 = (f32[256,512]{1,0:T(8,128)S(1)}) conditional(s32[]{:T(128)} %bitcast.85, f32[256,512]{1,0:T(8,128)S(1)} %get-tuple-element.814, (s32[]{:T(128)}, f32[7,256,256]{2,1,0:T(8,128)}, f32[7,256,256]{2,1,0:T(8,128)S(1)}, f32[]{:T(128)}, s32[7]{0:T(128)S(1)}, /*index=5*/s32[8,15,256]{2,1,0:T(8,128)S(1)}, f32[7]{0:T(128)S(1)}, ...), branch_computations={%region_13.13_spmd, %region_14.17_spmd} | conditional | flops 139329280 | bytes 5297766 | solution.py:99
  205.7 1.7 fusion.22
  207.4 1.3 fusion.15
  208.7 1.8 fusion.10
  211.8 7.2 %conditional.5 = (f32[256,512]{1,0:T(8,128)S(1)}) conditional(s32[]{:T(128)} %bitcast.85, f32[256,512]{1,0:T(8,128)S(1)} %get-tuple-element.814, (s32[]{:T(128)}, f32[7,256,256]{2,1,0:T(8,128)}, f32[7,256,256]{2,1,0:T(8,128)S(1)}, f32[]{:T(128)}, s32[7]{0:T(128)S(1)}, /*index=5*/s32[8,15,256]{2,1,0:T(8,128)S(1)}, f32[7]{0:T(128)S(1)}, ...), branch_computations={%region_13.13_spmd, %region_14.17_spmd} | conditional | flops 139329280 | bytes 5297766 | solution.py:99
  214.1 1.7 fusion.22
  215.9 1.3 fusion.15
  217.2 1.8 fusion.10
  220.3 7.2 %conditional.5 = (f32[256,512]{1,0:T(8,128)S(1)}) conditional(s32[]{:T(128)} %bitcast.85, f32[256,512]{1,0:T(8,128)S(1)} %get-tuple-element.814, (s32[]{:T(128)}, f32[7,256,256]{2,1,0:T(8,128)}, f32[7,256,256]{2,1,0:T(8,128)S(1)}, f32[]{:T(128)}, s32[7]{0:T(128)S(1)}, /*index=5*/s32[8,15,256]{2,1,0:T(8,128)S(1)}, f32[7]{0:T(128)S(1)}, ...), branch_computations={%region_13.13_spmd, %region_14.17_spmd} | conditional | flops 139329280 | bytes 5297766 | solution.py:99
  222.6 1.7 fusion.22
  224.4 1.3 fusion.15
  225.6 1.8 fusion.10
  228.7 7.2 %conditional.5 = (f32[256,512]{1,0:T(8,128)S(1)}) conditional(s32[]{:T(128)} %bitcast.85, f32[256,512]{1,0:T(8,128)S(1)} %get-tuple-element.814, (s32[]{:T(128)}, f32[7,256,256]{2,1,0:T(8,128)}, f32[7,256,256]{2,1,0:T(8,128)S(1)}, f32[]{:T(128)}, s32[7]{0:T(128)S(1)}, /*index=5*/s32[8,15,256]{2,1,0:T(8,128)S(1)}, f32[7]{0:T(128)S(1)}, ...), branch_computations={%region_13.13_spmd, %region_14.17_spmd} | conditional | flops 139329280 | bytes 5297766 | solution.py:99
  231.1 1.7 fusion.22
  232.8 1.3 fusion.15
  234.1 1.8 fusion.10
  237.2 7.2 %conditional.5 = (f32[256,512]{1,0:T(8,128)S(1)}) conditional(s32[]{:T(128)} %bitcast.85, f32[256,512]{1,0:T(8,128)S(1)} %get-tuple-element.814, (s32[]{:T(128)}, f32[7,256,256]{2,1,0:T(8,128)}, f32[7,256,256]{2,1,0:T(8,128)S(1)}, f32[]{:T(128)}, s32[7]{0:T(128)S(1)}, /*index=5*/s32[8,15,256]{2,1,0:T(8,128)S(1)}, f32[7]{0:T(128)S(1)}, ...), branch_computations={%region_13.13_spmd, %region_14.17_spmd} | conditional | flops 139329280 | bytes 5297766 | solution.py:99
  239.5 1.7 fusion.22
  241.3 1.3 fusion.15
  242.6 1.8 fusion.10
  245.6 7.2 %conditional.5 = (f32[256,512]{1,0:T(8,128)S(1)}) conditional(s32[]{:T(128)} %bitcast.85, f32[256,512]{1,0:T(8,128)S(1)} %get-tuple-element.814, (s32[]{:T(128)}, f32[7,256,256]{2,1,0:T(8,128)}, f32[7,256,256]{2,1,0:T(8,128)S(1)}, f32[]{:T(128)}, s32[7]{0:T(128)S(1)}, /*index=5*/s32[8,15,256]{2,1,0:T(8,128)S(1)}, f32[7]{0:T(128)S(1)}, ...), branch_computations={%region_13.13_spmd, %region_14.17_spmd} | conditional | flops 139329280 | bytes 5297766 | solution.py:99
  248.0 1.7 fusion.22
  249.7 1.3 fusion.15
  251.0 1.8 fusion.10
  (104 shorter events, 44.4 us)
Async XLA Ops:
  7.2 10.9 %copy-start.2 = (bf16[256,512]{1,0:T(8,128)(2,1)S(1)}, bf16[256,512]{1,0:T(8,128)(2,1)}, u32[]{:S(2)}) copy-start(bf16[256,512]{1,0:T(8,128)(2,1)} %param.12) | copy-start | bytes 786436
  7.2 11.0 %copy-start.4 = (s32[1,7]{1,0:T(1,128)S(1)}, s32[1,7]{1,0:T(1,128)}, u32[]{:S(2)}) copy-start(s32[1,7]{1,0:T(1,128)} %param.14) | copy-start | bytes 88
  7.2 54.8 %all-gather.2.cloned.1.call-start = ((), (), s32[]{:S(2)}) async-start(), calls=%async_computation.1 | async-start | bytes 2359296 | tf_op jit(solution)/shard_map/all_gather | solution.py:28
  9.8 183.8 %all-to-all-start = ((s32[8,15,256]{2,1,0:T(8,128)}), s32[8,15,256]{2,1,0:T(8,128)S(1)}, u32[]{:S(2)}, u32[]{:S(2)}) async-start(s32[8,15,256]{2,1,0:T(8,128)} %copy.16), calls=%async_computation | async-start | bytes 262144 | tf_op jit(solution)/shard_map/all_to_all | solution.py:79
  62.0 1.6 copy-start.3
  143.6 48.1 %copy-start.1 = (f32[7,256,256]{1,2,0:T(8,128)}, f32[7,256,256]{1,2,0:T(8,128)S(1)}, u32[]{:S(2)}) copy-start(f32[7,256,256]{1,2,0:T(8,128)S(1)} %get-tuple-element.528) | copy-start | bytes 5505028
  252.9 0.8 copy-start
Sparse Core Ops, SparseCore 0:
  10.1 51.8 all-gather.1
where the time goes:
time: 264 us; the launch traced here: 262 us
  waiting for transfers between devices  44.4 us (17%)
  blocking collectives  41.4 us (16%)
  matrix products  40.6 us (15%)
  other arithmetic  39.2 us (15%)
  local copies, waits for them, and re-layouts  38.7 us (15%)
  loops' own time  30.7 us (12%)
  between operations  19.2 us (7%)
  starting transfers between devices  7.32 us (3%)
    all_gather x1, waiting for transfers between devices, per_device(): lax.all_gather(embeddings, 'wide', axis=0, tiled=True)  43.7 us
    psum x1, blocking collectives, per_device(): lax.psum((kernel_sum, attract_sum, edge_sum, entry_sum), ('wide', 'narrow'))  41.4 us
    dot_general x7, matrix products, tile_kernel(): jnp.einsum('id,jd->ij', local_rows, remote_rows, preferred_element_type=j...  17.8 us
    another operation x7, loops' own time, first(): lax.cond(partner_row[slot] >= 0, first_active, lambda carry: carry, carry)  16.8 us
    dot_general x7, matrix products, second_active(): jnp.dot(mirror.astype(jnp.bfloat16), remote_rows, preferred_element_type=...  12.8 us
    reduce_sum x7, other arithmetic, second_active(): row_total = jnp.sum(weight, axis=1) + jnp.sum(mirror, axis=1)  12.2 us
    dynamic_update_slice x7, other arithmetic, first_active(): lax.dynamic_update_index_in_dim(counts_store, counts, slot, 0)  9.57 us
    dot_general x7, matrix products, second_active(): jnp.dot(weight.astype(jnp.bfloat16), remote_rows, preferred_element_type=...  8.86 us
  transfers between devices with their start and end apart: 2, of which 1 were waited for; matrix products, arithmetic and copies ran while one was open for 26% of the time, Pallas kernels for 0%

commit v1 on v0

--- a/solution.py
+++ b/solution.py
@@ -67,7 +67,7 @@
     )
     kernel_sum, attract_sum, edge_sum, entry_sum = sums
     total, attract, edges_total, entries = lax.psum(
-        (kernel_sum, attract_sum, edge_sum, entry_sum), ("wide", "narrow")
+        lax.psum((kernel_sum, attract_sum, edge_sum, entry_sum), "wide"), "narrow"
     )
     mean_loss = -attract / edges_total + jnp.log(total / entries)
     repulsion = edges_total / total

time: 264 us -> 249 us (0.943)
  blocking collectives: 41.4 us -> 26.4 us
    psum x1 -> x2, blocking collectives: 41.4 us -> 26.4 us  [the longest x1 20 us: per_device(): lax.psum((kernel_sum, attract_sum, edge_sum, entry_sum), 'wide')]
  transfers between devices with their start and end apart: 2 -> 2, of which waited for: 1 -> 1; matrix products, arithmetic and copies ran while one was open for 26% -> 28% of each run, Pallas kernels for 0% -> 0%
where the time goes in v1:
time: 249 us; the launch traced here: 247 us
  waiting for transfers between devices  44.4 us (18%)
  matrix products  40.6 us (16%)
  other arithmetic  39.2 us (16%)
  local copies, waits for them, and re-layouts  38.7 us (16%)
  loops' own time  30.7 us (12%)
  blocking collectives  26.4 us (11%)
  between operations  19.1 us (8%)
  starting transfers between devices  7.32 us (3%)
    all_gather x1, waiting for transfers between devices, per_device(): lax.all_gather(embeddings, 'wide', axis=0, tiled=True)  43.7 us
    psum x1, blocking collectives, per_device(): lax.psum((kernel_sum, attract_sum, edge_sum, entry_sum), 'wide')  20 us
    dot_general x7, matrix products, tile_kernel(): jnp.einsum('id,jd->ij', local_rows, remote_rows, preferred_element_type=j...  17.8 us
    another operation x7, loops' own time, first(): lax.cond(partner_row[slot] >= 0, first_active, lambda carry: carry, carry)  16.8 us
    dot_general x7, matrix products, second_active(): jnp.dot(mirror.astype(jnp.bfloat16), remote_rows, preferred_element_type=...  12.8 us
    reduce_sum x7, other arithmetic, second_active(): row_total = jnp.sum(weight, axis=1) + jnp.sum(mirror, axis=1)  12.2 us
    dynamic_update_slice x7, other arithmetic, first_active(): lax.dynamic_update_index_in_dim(counts_store, counts, slot, 0)  9.57 us
    dot_general x7, matrix products, second_active(): jnp.dot(weight.astype(jnp.bfloat16), remote_rows, preferred_element_type=...  8.86 us
  transfers between devices with their start and end apart: 2, of which 1 were waited for; matrix products, arithmetic and copies ran while one was open for 28% of the time, Pallas kernels for 0%

profile of v1, /device:TPU:0, one launch (start us, length us, event | category | flops | bytes accessed | tf_op | source)
XLA Modules:
  0.0 246.5 jit_solution(6365610034684461545)
XLA Ops:
  7.9 1.2 fusion.38
  9.8 7.3 %all-to-all-start = ((s32[8,15,256]{2,1,0:T(8,128)}), s32[8,15,256]{2,1,0:T(8,128)S(1)}, u32[]{:S(2)}, u32[]{:S(2)}) async-start(s32[8,15,256]{2,1,0:T(8,128)} %copy.16), calls=%async_computation | async-start | bytes 262144 | tf_op jit(solution)/shard_map/all_to_all | solution.py:79
  18.2 43.7 %all-gather.2.cloned.1.call-done = bf16[2048,512]{1,0:T(8,128)(2,1)} async-done(((bf16[256,512]{1,0:T(8,128)(2,1)}), bf16[2048,512]{1,0:T(8,128)(2,1)}) %all-gather.2.cloned.1.call-update) | async-done | bytes 2097168 | tf_op jit(solution)/shard_map/all_gather | solution.py:28
  62.1 1.4 broadcast_in_dim.17.clone
  63.5 80.1 %while.39 = (s32[]{:T(128)}, f32[]{:T(128)}, f32[]{:T(128)}, f32[]{:T(128)}, f32[]{:T(128)}, /*index=5*/f32[7,256,256]{1,2,0:T(8,128)S(1)}, f32[7,256,256]{1,2,0...) while((s32[]{:T(128)}, f32[]{:T(128)}, f32[]{:T(128)}, ...), condition=%wide.region_9.10_spmd, body=%wide.region_1.9_spmd.sunk | while | flops 71171840 | bytes 3196933 | solution.py:65
  64.8 10.2 %conditional.4 = ((f32[]{:T(128)}, f32[]{:T(128)}, f32[]{:T(128)}, f32[]{:T(128)}, f32[7,256,256]{1,2,0:T(8,128)S(1)}, /*index=5*/f32[7,256,256]{1,2,0:T(8,128)})) conditional(s32[]{:T(128)} %bitcast.84, (f32[]{:T(128)}, f32[]{:T(128)}, f32[]{:T(128)}, f32[]{:T(128)}, f32[7,256,256]{1,2,0:T(8,128)S(1)}, ...), branch_computations={%region_2.0_spmd, %region_3.8_spmd} | conditional | flops 71171840 | bytes 3196614 | solution.py:61
  65.9 1.1 multiply_reduce_fusion
  69.3 2.6 %multiply_reduce_fusion.2 = (f32[]{:T(128)}, f32[]{:T(128)}, f32[]{:T(128)}, f32[256,256]{0,1:T(8,128)S(1)}) fusion(f32[256,256]{0,1:T(8,128)S(1)} %copy.14, f32[]{:T(128)} %bitcast.4, bf16[256,512]{1,0:T(8,128)(2,1)S(1)} %get-tuple-element.439, bf16[8,256,512]{2,1,0:T(8,128)(2,1)} %get-tuple-element.436, s32[]{:T(128)} %bitcast, ...), kind=kOutput, calls=%fused_computation.13 | convolution fusion | flops 67829760 | bytes 1051660 | tf_op jit(solution)/shard_map/while/body/eval_jaxpr/cond/branch_1_fun/id,jd->ij/dot_general | solution.py:9
  71.8 1.4 bitcast_dynamic-update-slice_fusion
  76.2 10.2 %conditional.4 = ((f32[]{:T(128)}, f32[]{:T(128)}, f32[]{:T(128)}, f32[]{:T(128)}, f32[7,256,256]{1,2,0:T(8,128)S(1)}, /*index=5*/f32[7,256,256]{1,2,0:T(8,128)})) conditional(s32[]{:T(128)} %bitcast.84, (f32[]{:T(128)}, f32[]{:T(128)}, f32[]{:T(128)}, f32[]{:T(128)}, f32[7,256,256]{1,2,0:T(8,128)S(1)}, ...), branch_computations={%region_2.0_spmd, %region_3.8_spmd} | conditional | flops 71171840 | bytes 3196614 | solution.py:61
  77.4 1.1 multiply_reduce_fusion
  80.7 2.5 %multiply_reduce_fusion.2 = (f32[]{:T(128)}, f32[]{:T(128)}, f32[]{:T(128)}, f32[256,256]{0,1:T(8,128)S(1)}) fusion(f32[256,256]{0,1:T(8,128)S(1)} %copy.14, f32[]{:T(128)} %bitcast.4, bf16[256,512]{1,0:T(8,128)(2,1)S(1)} %get-tuple-element.439, bf16[8,256,512]{2,1,0:T(8,128)(2,1)} %get-tuple-element.436, s32[]{:T(128)} %bitcast, ...), kind=kOutput, calls=%fused_computation.13 | convolution fusion | flops 67829760 | bytes 1051660 | tf_op jit(solution)/shard_map/while/body/eval_jaxpr/cond/branch_1_fun/id,jd->ij/dot_general | solution.py:9
  83.3 1.3 bitcast_dynamic-update-slice_fusion
  87.6 10.2 %conditional.4 = ((f32[]{:T(128)}, f32[]{:T(128)}, f32[]{:T(128)}, f32[]{:T(128)}, f32[7,256,256]{1,2,0:T(8,128)S(1)}, /*index=5*/f32[7,256,256]{1,2,0:T(8,128)})) conditional(s32[]{:T(128)} %bitcast.84, (f32[]{:T(128)}, f32[]{:T(128)}, f32[]{:T(128)}, f32[]{:T(128)}, f32[7,256,256]{1,2,0:T(8,128)S(1)}, ...), branch_computations={%region_2.0_spmd, %region_3.8_spmd} | conditional | flops 71171840 | bytes 3196614 | solution.py:61
  88.8 1.1 multiply_reduce_fusion
  92.1 2.5 %multiply_reduce_fusion.2 = (f32[]{:T(128)}, f32[]{:T(128)}, f32[]{:T(128)}, f32[256,256]{0,1:T(8,128)S(1)}) fusion(f32[256,256]{0,1:T(8,128)S(1)} %copy.14, f32[]{:T(128)} %bitcast.4, bf16[256,512]{1,0:T(8,128)(2,1)S(1)} %get-tuple-element.439, bf16[8,256,512]{2,1,0:T(8,128)(2,1)} %get-tuple-element.436, s32[]{:T(128)} %bitcast, ...), kind=kOutput, calls=%fused_computation.13 | convolution fusion | flops 67829760 | bytes 1051660 | tf_op jit(solution)/shard_map/while/body/eval_jaxpr/cond/branch_1_fun/id,jd->ij/dot_general | solution.py:9
  94.7 1.4 bitcast_dynamic-update-slice_fusion
  99.1 10.2 %conditional.4 = ((f32[]{:T(128)}, f32[]{:T(128)}, f32[]{:T(128)}, f32[]{:T(128)}, f32[7,256,256]{1,2,0:T(8,128)S(1)}, /*index=5*/f32[7,256,256]{1,2,0:T(8,128)})) conditional(s32[]{:T(128)} %bitcast.84, (f32[]{:T(128)}, f32[]{:T(128)}, f32[]{:T(128)}, f32[]{:T(128)}, f32[7,256,256]{1,2,0:T(8,128)S(1)}, ...), branch_computations={%region_2.0_spmd, %region_3.8_spmd} | conditional | flops 71171840 | bytes 3196614 | solution.py:61
  100.2 1.1 multiply_reduce_fusion
  103.6 2.5 %multiply_reduce_fusion.2 = (f32[]{:T(128)}, f32[]{:T(128)}, f32[]{:T(128)}, f32[256,256]{0,1:T(8,128)S(1)}) fusion(f32[256,256]{0,1:T(8,128)S(1)} %copy.14, f32[]{:T(128)} %bitcast.4, bf16[256,512]{1,0:T(8,128)(2,1)S(1)} %get-tuple-element.439, bf16[8,256,512]{2,1,0:T(8,128)(2,1)} %get-tuple-element.436, s32[]{:T(128)} %bitcast, ...), kind=kOutput, calls=%fused_computation.13 | convolution fusion | flops 67829760 | bytes 1051660 | tf_op jit(solution)/shard_map/while/body/eval_jaxpr/cond/branch_1_fun/id,jd->ij/dot_general | solution.py:9
  106.1 1.4 bitcast_dynamic-update-slice_fusion
  110.5 10.2 %conditional.4 = ((f32[]{:T(128)}, f32[]{:T(128)}, f32[]{:T(128)}, f32[]{:T(128)}, f32[7,256,256]{1,2,0:T(8,128)S(1)}, /*index=5*/f32[7,256,256]{1,2,0:T(8,128)})) conditional(s32[]{:T(128)} %bitcast.84, (f32[]{:T(128)}, f32[]{:T(128)}, f32[]{:T(128)}, f32[]{:T(128)}, f32[7,256,256]{1,2,0:T(8,128)S(1)}, ...), branch_computations={%region_2.0_spmd, %region_3.8_spmd} | conditional | flops 71171840 | bytes 3196614 | solution.py:61
  111.7 1.1 multiply_reduce_fusion
  115.0 2.5 %multiply_reduce_fusion.2 = (f32[]{:T(128)}, f32[]{:T(128)}, f32[]{:T(128)}, f32[256,256]{0,1:T(8,128)S(1)}) fusion(f32[256,256]{0,1:T(8,128)S(1)} %copy.14, f32[]{:T(128)} %bitcast.4, bf16[256,512]{1,0:T(8,128)(2,1)S(1)} %get-tuple-element.439, bf16[8,256,512]{2,1,0:T(8,128)(2,1)} %get-tuple-element.436, s32[]{:T(128)} %bitcast, ...), kind=kOutput, calls=%fused_computation.13 | convolution fusion | flops 67829760 | bytes 1051660 | tf_op jit(solution)/shard_map/while/body/eval_jaxpr/cond/branch_1_fun/id,jd->ij/dot_general | solution.py:9
  117.6 1.4 bitcast_dynamic-update-slice_fusion
  122.0 10.2 %conditional.4 = ((f32[]{:T(128)}, f32[]{:T(128)}, f32[]{:T(128)}, f32[]{:T(128)}, f32[7,256,256]{1,2,0:T(8,128)S(1)}, /*index=5*/f32[7,256,256]{1,2,0:T(8,128)})) conditional(s32[]{:T(128)} %bitcast.84, (f32[]{:T(128)}, f32[]{:T(128)}, f32[]{:T(128)}, f32[]{:T(128)}, f32[7,256,256]{1,2,0:T(8,128)S(1)}, ...), branch_computations={%region_2.0_spmd, %region_3.8_spmd} | conditional | flops 71171840 | bytes 3196614 | solution.py:61
  126.5 2.6 %multiply_reduce_fusion.2 = (f32[]{:T(128)}, f32[]{:T(128)}, f32[]{:T(128)}, f32[256,256]{0,1:T(8,128)S(1)}) fusion(f32[256,256]{0,1:T(8,128)S(1)} %copy.14, f32[]{:T(128)} %bitcast.4, bf16[256,512]{1,0:T(8,128)(2,1)S(1)} %get-tuple-element.439, bf16[8,256,512]{2,1,0:T(8,128)(2,1)} %get-tuple-element.436, s32[]{:T(128)} %bitcast, ...), kind=kOutput, calls=%fused_computation.13 | convolution fusion | flops 67829760 | bytes 1051660 | tf_op jit(solution)/shard_map/while/body/eval_jaxpr/cond/branch_1_fun/id,jd->ij/dot_general | solution.py:9
  129.0 1.4 bitcast_dynamic-update-slice_fusion
  133.4 10.2 %conditional.4 = ((f32[]{:T(128)}, f32[]{:T(128)}, f32[]{:T(128)}, f32[]{:T(128)}, f32[7,256,256]{1,2,0:T(8,128)S(1)}, /*index=5*/f32[7,256,256]{1,2,0:T(8,128)})) conditional(s32[]{:T(128)} %bitcast.84, (f32[]{:T(128)}, f32[]{:T(128)}, f32[]{:T(128)}, f32[]{:T(128)}, f32[7,256,256]{1,2,0:T(8,128)S(1)}, ...), branch_computations={%region_2.0_spmd, %region_3.8_spmd} | conditional | flops 71171840 | bytes 3196614 | solution.py:61
  137.9 2.5 %multiply_reduce_fusion.2 = (f32[]{:T(128)}, f32[]{:T(128)}, f32[]{:T(128)}, f32[256,256]{0,1:T(8,128)S(1)}) fusion(f32[256,256]{0,1:T(8,128)S(1)} %copy.14, f32[]{:T(128)} %bitcast.4, bf16[256,512]{1,0:T(8,128)(2,1)S(1)} %get-tuple-element.439, bf16[8,256,512]{2,1,0:T(8,128)(2,1)} %get-tuple-element.436, s32[]{:T(128)} %bitcast, ...), kind=kOutput, calls=%fused_computation.13 | convolution fusion | flops 67829760 | bytes 1051660 | tf_op jit(solution)/shard_map/while/body/eval_jaxpr/cond/branch_1_fun/id,jd->ij/dot_general | solution.py:9
  140.5 1.4 bitcast_dynamic-update-slice_fusion
  143.6 20.0 %all-reduce = (f32[]{:T(128)}, f32[]{:T(128)}, f32[]{:T(128)}, f32[]{:T(128)}) all-reduce(f32[]{:T(128)} %get-tuple-element.499, f32[]{:T(128)} %get-tuple-element.500, f32[]{:T(128)} %get-tuple-element.502, f32[]{:T(128)} %get-tuple-element.503), channel_id=1, replica_groups=mesh['wide'=8,'narrow'=4] {'wide'}, use_global_device_ids=true, to_apply=%region_10.11 | all-reduce | flops 4 | bytes 32 | tf_op jit(solution)/shard_map/psum | solution.py:70
  163.7 6.3 %all-reduce.1 = (f32[]{:T(128)}, f32[]{:T(128)}, f32[]{:T(128)}, f32[]{:T(128)}) all-reduce(f32[]{:T(128)} %get-tuple-element.585, f32[]{:T(128)} %get-tuple-element.586, f32[]{:T(128)} %get-tuple-element.587, f32[]{:T(128)} %get-tuple-element.588), channel_id=1, replica_groups=mesh['wide'=8,'narrow'=4] {'narrow'}, use_global_device_ids=true, to_apply=%region_11.12 | all-reduce | flops 4 | bytes 32 | tf_op jit(solution)/shard_map/psum | solution.py:69
  173.9 2.7 %copy.17 = f32[7,256,256]{2,1,0:T(8,128)} copy(f32[7,256,256]{1,2,0:T(8,128)} %get-tuple-element.527) | data formatting | bytes 3670016 | tf_op jit(solution)/shard_map/while | solution.py:101
  176.6 1.8 copy.18
  178.5 59.2 %while.40 = (s32[]{:T(128)}, f32[256,512]{1,0:T(8,128)S(1)}, s32[7]{0:T(128)S(1)}, f32[7,256,256]{2,1,0:T(8,128)}, f32[7,256,256]{2,1,0:T(8,128)S(1)}, /*index=5...) while((s32[]{:T(128)}, f32[256,512]{1,0:T(8,128)S(1)}, ...), condition=%wide.region_20.21_spmd, body=%wide.region_14.20_spmd.sunk | while | flops 139329280 | bytes 5297989 | solution.py:101
  179.8 7.2 %conditional.5 = (f32[256,512]{1,0:T(8,128)S(1)}) conditional(s32[]{:T(128)} %bitcast.85, f32[256,512]{1,0:T(8,128)S(1)} %get-tuple-element.818, (s32[]{:T(128)}, f32[7,256,256]{2,1,0:T(8,128)}, f32[7,256,256]{2,1,0:T(8,128)S(1)}, f32[]{:T(128)}, s32[7]{0:T(128)S(1)}, /*index=5*/s32[8,15,256]{2,1,0:T(8,128)S(1)}, f32[7]{0:T(128)S(1)}, ...), branch_computations={%region_15.15_spmd, %region_16.19_spmd} | conditional | flops 139329280 | bytes 5297766 | solution.py:99
  182.1 1.7 fusion.22
  183.9 1.3 fusion.15
  185.1 1.8 fusion.10
  188.2 7.2 %conditional.5 = (f32[256,512]{1,0:T(8,128)S(1)}) conditional(s32[]{:T(128)} %bitcast.85, f32[256,512]{1,0:T(8,128)S(1)} %get-tuple-element.818, (s32[]{:T(128)}, f32[7,256,256]{2,1,0:T(8,128)}, f32[7,256,256]{2,1,0:T(8,128)S(1)}, f32[]{:T(128)}, s32[7]{0:T(128)S(1)}, /*index=5*/s32[8,15,256]{2,1,0:T(8,128)S(1)}, f32[7]{0:T(128)S(1)}, ...), branch_computations={%region_15.15_spmd, %region_16.19_spmd} | conditional | flops 139329280 | bytes 5297766 | solution.py:99
  190.6 1.7 fusion.22
  192.3 1.3 fusion.15
  193.6 1.8 fusion.10
  196.7 7.2 %conditional.5 = (f32[256,512]{1,0:T(8,128)S(1)}) conditional(s32[]{:T(128)} %bitcast.85, f32[256,512]{1,0:T(8,128)S(1)} %get-tuple-element.818, (s32[]{:T(128)}, f32[7,256,256]{2,1,0:T(8,128)}, f32[7,256,256]{2,1,0:T(8,128)S(1)}, f32[]{:T(128)}, s32[7]{0:T(128)S(1)}, /*index=5*/s32[8,15,256]{2,1,0:T(8,128)S(1)}, f32[7]{0:T(128)S(1)}, ...), branch_computations={%region_15.15_spmd, %region_16.19_spmd} | conditional | flops 139329280 | bytes 5297766 | solution.py:99
  199.0 1.7 fusion.22
  200.8 1.3 fusion.15
  202.0 1.8 fusion.10
  205.1 7.2 %conditional.5 = (f32[256,512]{1,0:T(8,128)S(1)}) conditional(s32[]{:T(128)} %bitcast.85, f32[256,512]{1,0:T(8,128)S(1)} %get-tuple-element.818, (s32[]{:T(128)}, f32[7,256,256]{2,1,0:T(8,128)}, f32[7,256,256]{2,1,0:T(8,128)S(1)}, f32[]{:T(128)}, s32[7]{0:T(128)S(1)}, /*index=5*/s32[8,15,256]{2,1,0:T(8,128)S(1)}, f32[7]{0:T(128)S(1)}, ...), branch_computations={%region_15.15_spmd, %region_16.19_spmd} | conditional | flops 139329280 | bytes 5297766 | solution.py:99
  207.5 1.7 fusion.22
  209.2 1.3 fusion.15
  210.5 1.8 fusion.10
  213.6 7.2 %conditional.5 = (f32[256,512]{1,0:T(8,128)S(1)}) conditional(s32[]{:T(128)} %bitcast.85, f32[256,512]{1,0:T(8,128)S(1)} %get-tuple-element.818, (s32[]{:T(128)}, f32[7,256,256]{2,1,0:T(8,128)}, f32[7,256,256]{2,1,0:T(8,128)S(1)}, f32[]{:T(128)}, s32[7]{0:T(128)S(1)}, /*index=5*/s32[8,15,256]{2,1,0:T(8,128)S(1)}, f32[7]{0:T(128)S(1)}, ...), branch_computations={%region_15.15_spmd, %region_16.19_spmd} | conditional | flops 139329280 | bytes 5297766 | solution.py:99
  215.9 1.7 fusion.22
  217.7 1.3 fusion.15
  219.0 1.8 fusion.10
  222.1 7.2 %conditional.5 = (f32[256,512]{1,0:T(8,128)S(1)}) conditional(s32[]{:T(128)} %bitcast.85, f32[256,512]{1,0:T(8,128)S(1)} %get-tuple-element.818, (s32[]{:T(128)}, f32[7,256,256]{2,1,0:T(8,128)}, f32[7,256,256]{2,1,0:T(8,128)S(1)}, f32[]{:T(128)}, s32[7]{0:T(128)S(1)}, /*index=5*/s32[8,15,256]{2,1,0:T(8,128)S(1)}, f32[7]{0:T(128)S(1)}, ...), branch_computations={%region_15.15_spmd, %region_16.19_spmd} | conditional | flops 139329280 | bytes 5297766 | solution.py:99
  224.4 1.7 fusion.22
  226.2 1.3 fusion.15
  227.4 1.8 fusion.10
  230.5 7.2 %conditional.5 = (f32[256,512]{1,0:T(8,128)S(1)}) conditional(s32[]{:T(128)} %bitcast.85, f32[256,512]{1,0:T(8,128)S(1)} %get-tuple-element.818, (s32[]{:T(128)}, f32[7,256,256]{2,1,0:T(8,128)}, f32[7,256,256]{2,1,0:T(8,128)S(1)}, f32[]{:T(128)}, s32[7]{0:T(128)S(1)}, /*index=5*/s32[8,15,256]{2,1,0:T(8,128)S(1)}, f32[7]{0:T(128)S(1)}, ...), branch_computations={%region_15.15_spmd, %region_16.19_spmd} | conditional | flops 139329280 | bytes 5297766 | solution.py:99
  232.9 1.7 fusion.22
  234.6 1.3 fusion.15
  235.9 1.8 fusion.10
  (105 shorter events, 45.5 us)
Async XLA Ops:
  7.2 10.9 %copy-start.2 = (bf16[256,512]{1,0:T(8,128)(2,1)S(1)}, bf16[256,512]{1,0:T(8,128)(2,1)}, u32[]{:S(2)}) copy-start(bf16[256,512]{1,0:T(8,128)(2,1)} %param.12) | copy-start | bytes 786436
  7.2 11.0 %copy-start.4 = (s32[1,7]{1,0:T(1,128)S(1)}, s32[1,7]{1,0:T(1,128)}, u32[]{:S(2)}) copy-start(s32[1,7]{1,0:T(1,128)} %param.14) | copy-start | bytes 88
  7.2 54.8 %all-gather.2.cloned.1.call-start = ((), (), s32[]{:S(2)}) async-start(), calls=%async_computation.1 | async-start | bytes 2359296 | tf_op jit(solution)/shard_map/all_gather | solution.py:28
  9.8 168.6 %all-to-all-start = ((s32[8,15,256]{2,1,0:T(8,128)}), s32[8,15,256]{2,1,0:T(8,128)S(1)}, u32[]{:S(2)}, u32[]{:S(2)}) async-start(s32[8,15,256]{2,1,0:T(8,128)} %copy.16), calls=%async_computation | async-start | bytes 262144 | tf_op jit(solution)/shard_map/all_to_all | solution.py:79
  62.0 1.6 copy-start.3
  143.6 33.0 %copy-start.1 = (f32[7,256,256]{1,2,0:T(8,128)}, f32[7,256,256]{1,2,0:T(8,128)S(1)}, u32[]{:S(2)}) copy-start(f32[7,256,256]{1,2,0:T(8,128)S(1)} %get-tuple-element.528) | copy-start | bytes 5505028
  237.7 0.8 copy-start
Sparse Core Ops, SparseCore 0:
  10.1 51.8 all-gather.1
